TPU v7x, 256 devices: a whole 4x4x8 slice. The times are simulated.
256 devices in a mesh: leaf: 8 (over x, core), row: 32 (over y, z).
Axes of the slice: x: 4, y: 4, z: 8, core: 2. Of those that a mesh axis runs over, the one named last changes fastest.
Arguments:
- loc_rhs: float32 [8, 32, 512, 128], P('leaf', 'row'), may hold values from -6 to 6
- loc_inverse: float32 [8, 32, 512, 512], P('leaf', 'row'), may hold values from -0.25 to 0.25
- loc_coupling: float32 [8, 32, 512, 512], P('leaf', 'row'), may hold values from -0.09375 to 0.09375
- loc_pivots: float32 [8, 32, 512], P('leaf', 'row'), may hold values from 0.5 to 4
- pattern: int32 [8, 32, 4], P('leaf', 'row'), may hold values from 0 to 29, as said below
- win_rhs: float32 [4, 2048, 128], P(None, ('leaf', 'row')), may hold values from -6 to 6
- win_pivots: float32 [4, 2048], P(None, ('leaf', 'row')), may hold values from 0.5 to 4
- win_inverse: float32 [32, 120, 2048], P('row', None, 'leaf'), may hold values from -0.125 to 0.125
- win_coupling: float32 [32, 112, 2048], P('row', None, 'leaf'), may hold values from -0.125 to 0.125
Outputs:
- loc_solution: float32 [8, 32, 512, 128], P('leaf', 'row')
- win_solution: float32 [4, 2048, 128], P(None, ('leaf', 'row'))
Inputs may be any that keep to these rules, and one draw needn't show every extreme that they name: `pattern`: on each device the 4 tile numbers are distinct; number p stands for rows p * 128 to (p + 1) * 128 - 1 of the path of the device's leaf index.
All inputs are finite; a program needn't handle non-finite values.
Results may differ from a plain program's by a relative error of at most 0.0001.
Values sent between devices are 32-bit elements; how exact they have to be, the bound alone decides.
A program may use at most 64 MiB of HBM per device.

v0:
```python
import jax
import jax.numpy as jnp
from jax import lax
from jax.sharding import PartitionSpec as P

BASE = 256
TILE = 128
PRECISE = lax.Precision.HIGHEST


def contract_first(left, right):
    return lax.dot_general(left, right, (((0,), (0,)), ((), ())), precision=PRECISE)


def group_sum(partial_value, height, leaf_id, leaf_count):
    group_span = 2**height
    if group_span == 1:
        return partial_value[0]
    padded = jnp.zeros((leaf_count,) + partial_value.shape[1:], jnp.float32)
    padded = lax.dynamic_update_slice_in_dim(
        padded, partial_value, leaf_id // group_span * group_span, 0
    )
    return lax.psum_scatter(padded, "leaf", scatter_dimension=0, tiled=True)[0]


def group_gather(piece, height, leaf_id):
    group_span = 2**height
    if group_span == 1:
        return piece[None]
    whole_set = lax.all_gather(piece[None], "leaf", axis=0, tiled=True)
    return lax.dynamic_slice_in_dim(whole_set, leaf_id // group_span * group_span, group_span, 0)


def masked_block(diag_block, group_span, piece_rows, rank_id, leaf_id):
    row_ids = (
        jnp.arange(group_span)[:, None] * BASE
        + rank_id * piece_rows
        + jnp.arange(piece_rows)[None, :]
    ).reshape(-1)
    col_ids = leaf_id % group_span * BASE + jnp.arange(BASE)
    return jnp.where(col_ids[None, :] < row_ids[:, None], diag_block, 0.0)


def shards(
    loc_rhs,
    loc_inverse,
    loc_coupling,
    loc_pivots,
    pattern,
    win_rhs,
    win_pivots,
    win_inverse,
    win_coupling,
):
    leaf_count = lax.axis_size("leaf")
    rank_count = lax.axis_size("row")
    leaf_id = lax.axis_index("leaf")
    rank_id = lax.axis_index("row")
    levels = win_rhs.shape[0]
    piece_rows = win_rhs.shape[1]
    columns = win_rhs.shape[2]
    groups_total = 2 * leaf_count - 1
    tile_groups = BASE // TILE
    tile_pieces = TILE // piece_rows
    inverse = loc_inverse[0, 0]
    coupling = loc_coupling[0, 0]
    tile_count = coupling.shape[0] // TILE
    own_tiles = pattern[0, 0]
    positions = jnp.arange(inverse.shape[0])
    strict_low = jnp.where(positions[None, :] < positions[:, None], inverse, 0.0)
    solved_loc = loc_rhs[0, 0] + jnp.dot(strict_low, loc_rhs[0, 0], precision=PRECISE)
    loc_terms = jnp.dot(coupling, solved_loc, precision=PRECISE).reshape(
        tile_count, tile_pieces, piece_rows, columns
    )
    slot_ids = jnp.arange(groups_total)[:, None] * tile_groups + jnp.arange(tile_groups)[None, :]
    selector = (slot_ids[:, :, None] == own_tiles[None, None, :]).astype(jnp.float32)
    local_sums = []
    placed = jnp.einsum("ght,tsix->ghsix", selector, loc_terms, precision=PRECISE)
    placed = placed.reshape(groups_total, rank_count, piece_rows, columns)
    padded_levels = []
    for height in range(levels):
        group_span = 2**height
        padded = jnp.zeros((leaf_count, rank_count, piece_rows, columns), jnp.float32)
        segment = placed[group_span - 1 : 2 * group_span - 1]
        padded_levels.append(
            lax.dynamic_update_slice_in_dim(padded, segment, leaf_id // group_span * group_span, 0)
        )
    stacked = jnp.stack(padded_levels).reshape(levels, leaf_count * rank_count, piece_rows, columns)
    summed = lax.psum_scatter(stacked, ("leaf", "row"), scatter_dimension=1, tiled=True)
    for height in range(levels):
        local_sums.append(summed[height, 0])
    from_children = jnp.zeros((piece_rows, columns), jnp.float32)
    solved = []
    diagonals = []
    for height in range(levels):
        group_span = 2**height
        diag_block = win_inverse[
            0, (group_span - 1) * piece_rows : (2 * group_span - 1) * piece_rows
        ]
        strict = masked_block(diag_block, group_span, piece_rows, rank_id, leaf_id)
        diagonals.append(strict)
        residual = win_rhs[height] - local_sums[height] - from_children
        gathered = lax.all_gather(residual, "row", axis=0, tiled=True)
        partial_value = jnp.dot(strict, gathered, precision=PRECISE).reshape(
            group_span, piece_rows, columns
        )
        current = residual + group_sum(partial_value, height, leaf_id, leaf_count)
        solved.append(current)
        if height + 1 < levels:
            spread = lax.all_gather(current, "row", axis=0, tiled=True)
            link_block = win_coupling[
                0, (2 * group_span - 2) * piece_rows : (4 * group_span - 2) * piece_rows
            ]
            coupled = jnp.dot(link_block, spread, precision=PRECISE).reshape(
                2 * group_span, piece_rows, columns
            )
            from_children = group_sum(coupled, height + 1, leaf_id, leaf_count)
    from_parent = jnp.zeros((piece_rows, columns), jnp.float32)
    results = [None] * levels
    spreads = [None] * levels
    for height in reversed(range(levels)):
        group_span = 2**height
        wanted = solved[height] / win_pivots[height][:, None] - from_parent
        rows_in = group_gather(wanted, height, leaf_id)
        partial_value = contract_first(
            diagonals[height], rows_in.reshape(group_span * piece_rows, columns)
        )
        current = wanted + lax.psum_scatter(partial_value, "row", scatter_dimension=0, tiled=True)
        results[height] = current
        spreads[height] = group_gather(current, height, leaf_id)
        if height > 0:
            child_span = group_span // 2
            link_block = win_coupling[
                0, (2 * child_span - 2) * piece_rows : (4 * child_span - 2) * piece_rows
            ]
            partial_value = contract_first(
                link_block, spreads[height].reshape(group_span * piece_rows, columns)
            )
            from_parent = lax.psum_scatter(partial_value, "row", scatter_dimension=0, tiled=True)
    stacked_out = jnp.stack(results)[:, None]
    whole_set = lax.all_gather(stacked_out, ("leaf", "row"), axis=1, tiled=True)
    whole_set = whole_set.reshape(levels, leaf_count, rank_count, piece_rows, columns)
    group_parts = []
    for height in range(levels):
        group_span = 2**height
        group_parts.append(
            lax.dynamic_slice_in_dim(
                whole_set[height], leaf_id // group_span * group_span, group_span, 0
            )
        )
    ordered = jnp.concatenate(group_parts, 0)
    ordered = ordered.reshape(groups_total, tile_groups, tile_pieces, piece_rows, columns)
    picked = jnp.einsum("ght,ghsix->tsix", selector, ordered, precision=PRECISE).reshape(
        tile_count * TILE, columns
    )
    scaled_loc = solved_loc / loc_pivots[0, 0][:, None]
    remainder = scaled_loc - contract_first(coupling, picked)
    answer = remainder + contract_first(strict_low, remainder)
    return (answer[None, None], jnp.stack(results))


def solution(mesh):
    return jax.shard_map(
        shards,
        mesh=mesh,
        in_specs=(
            P("leaf", "row", None, None),
            P("leaf", "row", None, None),
            P("leaf", "row", None, None),
            P("leaf", "row", None),
            P("leaf", "row", None),
            P(None, ("leaf", "row"), None),
            P(None, ("leaf", "row")),
            P("row", None, "leaf"),
            P("row", None, "leaf"),
        ),
        out_specs=(P("leaf", "row", None, None), P(None, ("leaf", "row"), None)),
        check_vma=False,
    )
```

profile of v0, /device:TPU:1, one launch (start us, length us, event | category | flops | bytes accessed | tf_op | source)
XLA Modules:
  0.0 1942.4 jit_solution(597287896424331740)
XLA Ops:
  7.3 2.3 convolution_add_fusion.1
  11.7 2.1 fusion.21
  19.7 2.2 pad_maximum_fusion
  23.4 271.0 %all-reduce.23.cloned.1.call-done = f32[4,256,8,128]{3,2,1,0:T(8,128)} async-done(((f32[4,256,8,128]{3,2,1,0:T(8,128)}), f32[4,256,8,128]{3,2,1,0:T(8,128)}) %all-reduce.23.cloned.1.call-update) | async-done | bytes 4194320
  295.1 34.5 %all_gather.42 = f32[256,128]{1,0:T(8,128)S(1)} all-gather(f32[8,128]{1,0:T(8,128)S(1)} %fusion.107), channel_id=1, replica_groups=mesh['leaf'=8,'row'=32] {'row'}, dimensions={0}, use_global_device_ids=true | all-gather | bytes 135168 | tf_op jit(solution)/shard_map/all_gather | solution.py:103
  329.8 32.6 %all_gather.43 = f32[256,128]{1,0:T(8,128)S(1)} all-gather(f32[8,128]{1,0:T(8,128)S(1)} %convolution_add_fusion.2), channel_id=1, replica_groups=mesh['leaf'=8,'row'=32] {'row'}, dimensions={0}, use_global_device_ids=true | all-gather | bytes 135168 | tf_op jit(solution)/shard_map/all_gather | solution.py:110
  362.5 38.8 %all-reduce.1 = f32[8,8,128]{2,1,0:T(8,128)S(1)} all-reduce(f32[8,8,128]{2,1,0:T(8,128)S(1)} %fusion.14), channel_id=9, replica_groups=mesh['leaf'=8,'row'=32] {'leaf'}, use_global_device_ids=true, to_apply=%region_1.2.clone | all-reduce | flops 8192 | bytes 65536
  402.7 32.9 %all_gather.44 = f32[256,128]{1,0:T(8,128)S(1)} all-gather(f32[8,128]{1,0:T(8,128)S(1)} %fusion.91), channel_id=1, replica_groups=mesh['leaf'=8,'row'=32] {'row'}, dimensions={0}, use_global_device_ids=true | all-gather | bytes 135168 | tf_op jit(solution)/shard_map/all_gather | solution.py:103
  435.8 33.1 %all-reduce.2 = f32[8,8,128]{2,1,0:T(8,128)S(1)} all-reduce(f32[8,8,128]{2,1,0:T(8,128)S(1)} %convolution_dynamic-update-slice_fusion.1), channel_id=10, replica_groups=mesh['leaf'=8,'row'=32] {'leaf'}, use_global_device_ids=true, to_apply=%region_2.3.clone | all-reduce | flops 8192 | bytes 65536
  469.6 30.8 %all_gather.45 = f32[256,128]{1,0:T(8,128)S(1)} all-gather(f32[8,128]{1,0:T(8,128)S(1)} %fusion.93), channel_id=1, replica_groups=mesh['leaf'=8,'row'=32] {'row'}, dimensions={0}, use_global_device_ids=true | all-gather | bytes 135168 | tf_op jit(solution)/shard_map/all_gather | solution.py:110
  500.6 33.7 %all-reduce.3 = f32[8,8,128]{2,1,0:T(8,128)S(1)} all-reduce(f32[8,8,128]{2,1,0:T(8,128)S(1)} %fusion.13), channel_id=11, replica_groups=mesh['leaf'=8,'row'=32] {'leaf'}, use_global_device_ids=true, to_apply=%region_3.4.clone | all-reduce | flops 8192 | bytes 65536
  535.7 32.2 %all_gather.46 = f32[256,128]{1,0:T(8,128)S(1)} all-gather(f32[8,128]{1,0:T(8,128)S(1)} %fusion.95), channel_id=1, replica_groups=mesh['leaf'=8,'row'=32] {'row'}, dimensions={0}, use_global_device_ids=true | all-gather | bytes 135168 | tf_op jit(solution)/shard_map/all_gather | solution.py:103
  568.2 33.7 %all-reduce.4 = f32[8,8,128]{2,1,0:T(8,128)S(1)} all-reduce(f32[8,8,128]{2,1,0:T(8,128)S(1)} %convolution_dynamic-update-slice_fusion), channel_id=12, replica_groups=mesh['leaf'=8,'row'=32] {'leaf'}, use_global_device_ids=true, to_apply=%region_4.5.clone | all-reduce | flops 8192 | bytes 65536
  602.5 30.8 %all_gather.47 = f32[256,128]{1,0:T(8,128)S(1)} all-gather(f32[8,128]{1,0:T(8,128)S(1)} %fusion.97), channel_id=1, replica_groups=mesh['leaf'=8,'row'=32] {'row'}, dimensions={0}, use_global_device_ids=true | all-gather | bytes 135168 | tf_op jit(solution)/shard_map/all_gather | solution.py:110
  633.6 33.7 %all-reduce.5 = f32[8,8,128]{2,1,0:T(8,128)S(1)} all-reduce(f32[8,8,128]{2,1,0:T(8,128)S(1)} %convolution_bitcast_fusion.5), channel_id=13, replica_groups=mesh['leaf'=8,'row'=32] {'leaf'}, use_global_device_ids=true, to_apply=%region_5.6.clone | all-reduce | flops 8192 | bytes 65536
  668.6 32.2 %all_gather.48 = f32[256,128]{1,0:T(8,128)S(1)} all-gather(f32[8,128]{1,0:T(8,128)S(1)} %bitcast_subtract_fusion.1), channel_id=1, replica_groups=mesh['leaf'=8,'row'=32] {'row'}, dimensions={0}, use_global_device_ids=true | all-gather | bytes 135168 | tf_op jit(solution)/shard_map/all_gather | solution.py:103
  701.1 33.7 %all-reduce.6 = f32[8,8,128]{2,1,0:T(8,128)S(1)} all-reduce(f32[8,8,128]{2,1,0:T(8,128)S(1)} %fusion.25), channel_id=14, replica_groups=mesh['leaf'=8,'row'=32] {'leaf'}, use_global_device_ids=true, to_apply=%region_6.7.clone | all-reduce | flops 8192 | bytes 65536
  736.2 16.3 all_gather.49
  755.0 133.2 %all-reduce.25.cloned.1.call-done = f32[256,128]{1,0:T(8,128)} async-done(((f32[256,128]{1,0:T(8,128)}), f32[256,128]{1,0:T(8,128)}) %all-reduce.25.cloned.1.call-update) | async-done | bytes 131088
  889.6 18.0 all-gather
  908.8 135.5 %all-reduce.27.cloned.1.call-done = f32[256,128]{1,0:T(8,128)} async-done(((f32[256,128]{1,0:T(8,128)}), f32[256,128]{1,0:T(8,128)}) %all-reduce.27.cloned.1.call-update) | async-done | bytes 131088
  1045.0 18.0 all-gather.1
  1064.2 135.5 %all-reduce.29.cloned.1.call-done = f32[256,128]{1,0:T(8,128)} async-done(((f32[256,128]{1,0:T(8,128)}), f32[256,128]{1,0:T(8,128)}) %all-reduce.29.cloned.1.call-update) | async-done | bytes 131088
  1200.4 18.0 all-gather.2
  1219.7 135.5 %all-reduce.31.cloned.1.call-done = f32[256,128]{1,0:T(8,128)} async-done(((f32[256,128]{1,0:T(8,128)}), f32[256,128]{1,0:T(8,128)}) %all-reduce.31.cloned.1.call-update) | async-done | bytes 131088
  1355.9 18.0 all-gather.3
  1375.1 135.5 %all-reduce.33.cloned.1.call-done = f32[256,128]{1,0:T(8,128)} async-done(((f32[256,128]{1,0:T(8,128)}), f32[256,128]{1,0:T(8,128)}) %all-reduce.33.cloned.1.call-update) | async-done | bytes 131088
  1511.3 18.0 all-gather.4
  1530.4 135.5 %all-reduce.35.cloned.1.call-done = f32[256,128]{1,0:T(8,128)} async-done(((f32[256,128]{1,0:T(8,128)}), f32[256,128]{1,0:T(8,128)}) %all-reduce.35.cloned.1.call-update) | async-done | bytes 131088
  1667.9 143.1 %all-reduce.37.cloned.1.call-done = f32[256,128]{1,0:T(8,128)} async-done(((f32[256,128]{1,0:T(8,128)}), f32[256,128]{1,0:T(8,128)}) %all-reduce.37.cloned.1.call-update) | async-done | bytes 131088
  1812.3 114.2 %all-gather.8.cloned.1.call-done = f32[4,2048,128]{2,1,0:T(8,128)} async-done(((f32[4,8,128]{2,1,0:T(8,128)}), f32[4,2048,128]{2,1,0:T(8,128)}) %all-gather.8.cloned.1.call-update) | async-done | bytes 4194320 | tf_op jit(solution)/shard_map/all_gather | solution.py:141
  1926.5 2.5 fusion.140
  (117 shorter events, 40.2 us)
Async XLA Ops:
  7.2 2.4 copy-start
  7.2 287.2 %all-reduce.23.cloned.1.call-start = ((), (), s32[]{:S(2)}) async-start(), calls=%async_computation.1 | async-start | bytes 8388608
  16.8 2.7 copy-start.2
  21.9 0.7 copy-start.10
  21.9 1.5 copy-start.6
  21.9 272.5 %copy-start.5 = (f32[4,8,128]{2,1,0:T(8,128)S(1)}, f32[4,8,128]{2,1,0:T(8,128)}, u32[]{:S(2)}) copy-start(f32[4,8,128]{2,1,0:T(8,128)} %param.14) | copy-start | bytes 49156
  22.0 307.6 %copy-start.3 = (f32[1,120,256]{2,1,0:T(8,128)S(1)}, f32[1,120,256]{2,1,0:T(8,128)}, u32[]{:S(2)}) copy-start(f32[1,120,256]{2,1,0:T(8,128)} %param.16) | copy-start | bytes 368644
  22.0 340.4 %copy-start.4 = (f32[1,112,256]{2,1,0:T(8,128)S(1)}, f32[1,112,256]{2,1,0:T(8,128)}, u32[]{:S(2)}) copy-start(f32[1,112,256]{2,1,0:T(8,128)} %param.17) | copy-start | bytes 344068
  22.0 731.9 %copy-start.9 = (u32[256]{0:T(256)S(1)}, u32[256]{0:T(256)}, u32[]{:S(2)}) copy-start(u32[256]{0:T(256)} %constant.167) | copy-start | bytes 3076
  22.0 866.2 %all-reduce.25.cloned.1.call-start = ((), (), s32[]{:S(2)}) async-start(), calls=%async_computation.2 | async-start | bytes 262144
  753.6 290.7 %all-reduce.27.cloned.1.call-start = ((), (), s32[]{:S(2)}) async-start(), calls=%async_computation.3 | async-start | bytes 262144
  908.7 291.1 %all-reduce.29.cloned.1.call-start = ((), (), s32[]{:S(2)}) async-start(), calls=%async_computation.4 | async-start | bytes 262144
  1064.2 291.0 %all-reduce.31.cloned.1.call-start = ((), (), s32[]{:S(2)}) async-start(), calls=%async_computation.5 | async-start | bytes 262144
  1219.5 291.1 %all-reduce.33.cloned.1.call-start = ((), (), s32[]{:S(2)}) async-start(), calls=%async_computation.6 | async-start | bytes 262144
  1375.0 291.0 %all-reduce.35.cloned.1.call-start = ((), (), s32[]{:S(2)}) async-start(), calls=%async_computation.7 | async-start | bytes 262144
  1530.4 280.5 %all-reduce.37.cloned.1.call-start = ((), (), s32[]{:S(2)}) async-start(), calls=%async_computation.8 | async-start | bytes 262144
  1667.8 258.7 %all-gather.8.cloned.1.call-start = ((), (), s32[]{:S(2)}) async-start(), calls=%async_computation | async-start | bytes 4210688 | tf_op jit(solution)/shard_map/all_gather | solution.py:141
  1929.0 1.5 copy-start.8
  1929.1 3.0 copy-start.7
  1930.0 3.9 copy-start.1
Sparse Core Ops, SparseCore 0:
  22.1 272.2 all-reduce.22
  753.7 134.3 all-reduce.24
  908.8 135.4 all-reduce.26
  1064.3 135.4 all-reduce.28
  1219.7 135.4 all-reduce.30
  1375.1 135.4 all-reduce.32
  1530.5 135.4 all-reduce.34
  1670.0 140.8 all-reduce.36
  1815.1 111.3 all-gather.7
where the time goes:
time: 1940 us
  waiting for transfers between devices  1340 us (69%)
  blocking collectives  539 us (28%)
    unnamed x17, waiting for transfers between devices  1220 us
    unnamed x6, blocking collectives  207 us
    all_gather x4, blocking collectives, shards(): gathered = lax.all_gather(residual, 'row', axis=0, tiled=True)  132 us
    all_gather x1, waiting for transfers between devices, shards(): whole_set = lax.all_gather(stacked_out, ('leaf', 'row'), axis=1, tiled=True)  114 us
    all_gather x6, blocking collectives, group_gather(): whole_set = lax.all_gather(piece[None], 'leaf', axis=0, tiled=True)  106 us
    all_gather x3, blocking collectives, shards(): spread = lax.all_gather(current, 'row', axis=0, tiled=True)  94.2 us
  transfers between devices with their start and end apart: 9, of which 9 were waited for; matrix products, arithmetic and copies ran while one was open for 0% of the time, Pallas kernels for 0%

commit v1 on v0

--- a/solution.py
+++ b/solution.py
@@ -138,7 +138,12 @@
             )
             from_parent = lax.psum_scatter(partial_value, "row", scatter_dimension=0, tiled=True)
     stacked_out = jnp.stack(results)[:, None]
-    whole_set = lax.all_gather(stacked_out, ("leaf", "row"), axis=1, tiled=True)
+    whole_set = jnp.concatenate(
+        lax.all_to_all(
+            jnp.stack([stacked_out] * lax.axis_size(("leaf", "row"))), ("leaf", "row"), 0, 0
+        ),
+        axis=1,
+    )
     whole_set = whole_set.reshape(levels, leaf_count, rank_count, piece_rows, columns)
     group_parts = []
     for height in range(levels):

time: 1940 us -> 1940 us (level)
  waiting for transfers between devices: 1340 us -> 1220 us
  blocking collectives: 539 us -> 651 us
    all_gather x1 -> x0, waiting for transfers between devices: 114 us -> none  [shards(): whole_set = lax.all_gather(stacked_out, ('leaf', 'row'), axis=1, tiled=True)]
    all_to_all x0 -> x1, blocking collectives: none -> 112 us  [shards(): lax.all_to_all(jnp.stack([stacked_out] * lax.axis_size(('leaf', 'row'))),...]
    unnamed x17 -> x16, waiting for transfers between devices: 1220 us -> 1220 us
  transfers between devices with their start and end apart: 9 -> 8, of which waited for: 9 -> 8; matrix products, arithmetic and copies ran while one was open for 0% -> 0% of each run, Pallas kernels for 0% -> 0%
where the time goes in v1:
time: 1940 us
  waiting for transfers between devices  1220 us (63%)
  blocking collectives  651 us (34%)
    unnamed x16, waiting for transfers between devices  1220 us
    unnamed x6, blocking collectives  207 us
    all_gather x4, blocking collectives, shards(): gathered = lax.all_gather(residual, 'row', axis=0, tiled=True)  132 us
    all_to_all x1, blocking collectives, shards(): lax.all_to_all(jnp.stack([stacked_out] * lax.axis_size(('leaf', 'row'))),...  112 us
    all_gather x6, blocking collectives, group_gather(): whole_set = lax.all_gather(piece[None], 'leaf', axis=0, tiled=True)  106 us
    all_gather x3, blocking collectives, shards(): spread = lax.all_gather(current, 'row', axis=0, tiled=True)  94.2 us
  transfers between devices with their start and end apart: 8, of which 8 were waited for; matrix products, arithmetic and copies ran while one was open for 0% of the time, Pallas kernels for 0%

profile of v1, /device:TPU:1, one launch (start us, length us, event | category | flops | bytes accessed | tf_op | source)
XLA Modules:
  0.0 1938.6 jit_solution(16705962793828648094)
XLA Ops:
  7.3 2.3 convolution_add_fusion.1
  11.7 2.1 fusion.21
  19.7 2.2 pad_maximum_fusion
  23.4 271.0 %all-reduce.23.cloned.1.call-done = f32[4,256,8,128]{3,2,1,0:T(8,128)} async-done(((f32[4,256,8,128]{3,2,1,0:T(8,128)}), f32[4,256,8,128]{3,2,1,0:T(8,128)}) %all-reduce.23.cloned.1.call-update) | async-done | bytes 4194320
  295.1 34.5 %all_gather.39 = f32[256,128]{1,0:T(8,128)S(1)} all-gather(f32[8,128]{1,0:T(8,128)S(1)} %fusion.107), channel_id=1, replica_groups=mesh['leaf'=8,'row'=32] {'row'}, dimensions={0}, use_global_device_ids=true | all-gather | bytes 135168 | tf_op jit(solution)/shard_map/all_gather | solution.py:103
  329.8 32.6 %all_gather.40 = f32[256,128]{1,0:T(8,128)S(1)} all-gather(f32[8,128]{1,0:T(8,128)S(1)} %convolution_add_fusion.2), channel_id=1, replica_groups=mesh['leaf'=8,'row'=32] {'row'}, dimensions={0}, use_global_device_ids=true | all-gather | bytes 135168 | tf_op jit(solution)/shard_map/all_gather | solution.py:110
  362.5 38.8 %all-reduce.1 = f32[8,8,128]{2,1,0:T(8,128)S(1)} all-reduce(f32[8,8,128]{2,1,0:T(8,128)S(1)} %fusion.14), channel_id=8, replica_groups=mesh['leaf'=8,'row'=32] {'leaf'}, use_global_device_ids=true, to_apply=%region_1.2.clone | all-reduce | flops 8192 | bytes 65536
  402.7 32.9 %all_gather.41 = f32[256,128]{1,0:T(8,128)S(1)} all-gather(f32[8,128]{1,0:T(8,128)S(1)} %fusion.91), channel_id=1, replica_groups=mesh['leaf'=8,'row'=32] {'row'}, dimensions={0}, use_global_device_ids=true | all-gather | bytes 135168 | tf_op jit(solution)/shard_map/all_gather | solution.py:103
  435.8 33.1 %all-reduce.2 = f32[8,8,128]{2,1,0:T(8,128)S(1)} all-reduce(f32[8,8,128]{2,1,0:T(8,128)S(1)} %convolution_dynamic-update-slice_fusion.1), channel_id=9, replica_groups=mesh['leaf'=8,'row'=32] {'leaf'}, use_global_device_ids=true, to_apply=%region_2.3.clone | all-reduce | flops 8192 | bytes 65536
  469.6 30.8 %all_gather.42 = f32[256,128]{1,0:T(8,128)S(1)} all-gather(f32[8,128]{1,0:T(8,128)S(1)} %fusion.93), channel_id=1, replica_groups=mesh['leaf'=8,'row'=32] {'row'}, dimensions={0}, use_global_device_ids=true | all-gather | bytes 135168 | tf_op jit(solution)/shard_map/all_gather | solution.py:110
  500.6 33.7 %all-reduce.3 = f32[8,8,128]{2,1,0:T(8,128)S(1)} all-reduce(f32[8,8,128]{2,1,0:T(8,128)S(1)} %fusion.13), channel_id=10, replica_groups=mesh['leaf'=8,'row'=32] {'leaf'}, use_global_device_ids=true, to_apply=%region_3.4.clone | all-reduce | flops 8192 | bytes 65536
  535.7 32.2 %all_gather.43 = f32[256,128]{1,0:T(8,128)S(1)} all-gather(f32[8,128]{1,0:T(8,128)S(1)} %fusion.95), channel_id=1, replica_groups=mesh['leaf'=8,'row'=32] {'row'}, dimensions={0}, use_global_device_ids=true | all-gather | bytes 135168 | tf_op jit(solution)/shard_map/all_gather | solution.py:103
  568.2 33.7 %all-reduce.4 = f32[8,8,128]{2,1,0:T(8,128)S(1)} all-reduce(f32[8,8,128]{2,1,0:T(8,128)S(1)} %convolution_dynamic-update-slice_fusion), channel_id=11, replica_groups=mesh['leaf'=8,'row'=32] {'leaf'}, use_global_device_ids=true, to_apply=%region_4.5.clone | all-reduce | flops 8192 | bytes 65536
  602.5 30.8 %all_gather.44 = f32[256,128]{1,0:T(8,128)S(1)} all-gather(f32[8,128]{1,0:T(8,128)S(1)} %fusion.97), channel_id=1, replica_groups=mesh['leaf'=8,'row'=32] {'row'}, dimensions={0}, use_global_device_ids=true | all-gather | bytes 135168 | tf_op jit(solution)/shard_map/all_gather | solution.py:110
  633.6 33.7 %all-reduce.5 = f32[8,8,128]{2,1,0:T(8,128)S(1)} all-reduce(f32[8,8,128]{2,1,0:T(8,128)S(1)} %convolution_bitcast_fusion.5), channel_id=12, replica_groups=mesh['leaf'=8,'row'=32] {'leaf'}, use_global_device_ids=true, to_apply=%region_5.6.clone | all-reduce | flops 8192 | bytes 65536
  668.6 32.2 %all_gather.45 = f32[256,128]{1,0:T(8,128)S(1)} all-gather(f32[8,128]{1,0:T(8,128)S(1)} %bitcast_subtract_fusion.1), channel_id=1, replica_groups=mesh['leaf'=8,'row'=32] {'row'}, dimensions={0}, use_global_device_ids=true | all-gather | bytes 135168 | tf_op jit(solution)/shard_map/all_gather | solution.py:103
  701.1 33.7 %all-reduce.6 = f32[8,8,128]{2,1,0:T(8,128)S(1)} all-reduce(f32[8,8,128]{2,1,0:T(8,128)S(1)} %fusion.25), channel_id=13, replica_groups=mesh['leaf'=8,'row'=32] {'leaf'}, use_global_device_ids=true, to_apply=%region_6.7.clone | all-reduce | flops 8192 | bytes 65536
  736.2 16.3 all_gather.46
  755.0 133.2 %all-reduce.25.cloned.1.call-done = f32[256,128]{1,0:T(8,128)} async-done(((f32[256,128]{1,0:T(8,128)}), f32[256,128]{1,0:T(8,128)}) %all-reduce.25.cloned.1.call-update) | async-done | bytes 131088
  889.6 18.0 all-gather
  908.8 135.5 %all-reduce.27.cloned.1.call-done = f32[256,128]{1,0:T(8,128)} async-done(((f32[256,128]{1,0:T(8,128)}), f32[256,128]{1,0:T(8,128)}) %all-reduce.27.cloned.1.call-update) | async-done | bytes 131088
  1045.0 18.0 all-gather.1
  1064.2 135.5 %all-reduce.29.cloned.1.call-done = f32[256,128]{1,0:T(8,128)} async-done(((f32[256,128]{1,0:T(8,128)}), f32[256,128]{1,0:T(8,128)}) %all-reduce.29.cloned.1.call-update) | async-done | bytes 131088
  1200.4 18.0 all-gather.2
  1219.7 135.5 %all-reduce.31.cloned.1.call-done = f32[256,128]{1,0:T(8,128)} async-done(((f32[256,128]{1,0:T(8,128)}), f32[256,128]{1,0:T(8,128)}) %all-reduce.31.cloned.1.call-update) | async-done | bytes 131088
  1355.9 18.0 all-gather.3
  1375.1 135.5 %all-reduce.33.cloned.1.call-done = f32[256,128]{1,0:T(8,128)} async-done(((f32[256,128]{1,0:T(8,128)}), f32[256,128]{1,0:T(8,128)}) %all-reduce.33.cloned.1.call-update) | async-done | bytes 131088
  1511.3 18.0 all-gather.4
  1530.4 135.5 %all-reduce.35.cloned.1.call-done = f32[256,128]{1,0:T(8,128)} async-done(((f32[256,128]{1,0:T(8,128)}), f32[256,128]{1,0:T(8,128)}) %all-reduce.35.cloned.1.call-update) | async-done | bytes 131088
  1667.8 143.1 %all-reduce.37.cloned.1.call-done = f32[256,128]{1,0:T(8,128)} async-done(((f32[256,128]{1,0:T(8,128)}), f32[256,128]{1,0:T(8,128)}) %all-reduce.37.cloned.1.call-update) | async-done | bytes 131088
  1812.2 112.1 %all_to_all.5 = f32[256,4,1,8,128]{4,3,2,1,0:T(8,128)S(1)} all-to-all(f32[256,4,1,8,128]{4,3,2,1,0:T(8,128)S(1)} %stack.51), channel_id=1, replica_groups=mesh['leaf'=8,'row'=32] {'leaf','row'}, dimensions={0} | all-to-all | bytes 8388608 | tf_op jit(solution)/shard_map/all_to_all | solution.py:142
  1929.8 1.9 fusion.8
  (119 shorter events, 38.7 us)
Async XLA Ops:
  7.2 2.4 copy-start
  7.2 287.2 %all-reduce.23.cloned.1.call-start = ((), (), s32[]{:S(2)}) async-start(), calls=%async_computation.1 | async-start | bytes 8388608
  16.8 2.7 copy-start.2
  21.9 0.7 copy-start.11
  21.9 1.5 copy-start.7
  21.9 272.5 %copy-start.6 = (f32[4,8,128]{2,1,0:T(8,128)S(1)}, f32[4,8,128]{2,1,0:T(8,128)}, u32[]{:S(2)}) copy-start(f32[4,8,128]{2,1,0:T(8,128)} %param.14) | copy-start | bytes 49156
  22.0 307.6 %copy-start.3 = (f32[1,120,256]{2,1,0:T(8,128)S(1)}, f32[1,120,256]{2,1,0:T(8,128)}, u32[]{:S(2)}) copy-start(f32[1,120,256]{2,1,0:T(8,128)} %param.16) | copy-start | bytes 368644
  22.0 340.4 %copy-start.4 = (f32[1,112,256]{2,1,0:T(8,128)S(1)}, f32[1,112,256]{2,1,0:T(8,128)}, u32[]{:S(2)}) copy-start(f32[1,112,256]{2,1,0:T(8,128)} %param.17) | copy-start | bytes 344068
  22.0 731.9 %copy-start.10 = (u32[256]{0:T(256)S(1)}, u32[256]{0:T(256)}, u32[]{:S(2)}) copy-start(u32[256]{0:T(256)} %constant.167) | copy-start | bytes 3076
  22.0 866.2 %all-reduce.25.cloned.1.call-start = ((), (), s32[]{:S(2)}) async-start(), calls=%async_computation.2 | async-start | bytes 262144
  753.6 290.7 %all-reduce.27.cloned.1.call-start = ((), (), s32[]{:S(2)}) async-start(), calls=%async_computation.3 | async-start | bytes 262144
  908.7 291.1 %all-reduce.29.cloned.1.call-start = ((), (), s32[]{:S(2)}) async-start(), calls=%async_computation.4 | async-start | bytes 262144
  1064.2 291.0 %all-reduce.31.cloned.1.call-start = ((), (), s32[]{:S(2)}) async-start(), calls=%async_computation.5 | async-start | bytes 262144
  1219.5 291.1 %all-reduce.33.cloned.1.call-start = ((), (), s32[]{:S(2)}) async-start(), calls=%async_computation.6 | async-start | bytes 262144
  1375.0 291.0 %all-reduce.35.cloned.1.call-start = ((), (), s32[]{:S(2)}) async-start(), calls=%async_computation.7 | async-start | bytes 262144
  1530.4 280.5 %all-reduce.37.cloned.1.call-start = ((), (), s32[]{:S(2)}) async-start(), calls=%async_computation.8 | async-start | bytes 262144
  1811.7 112.7 %copy-start.5 = (f32[4,8,128]{2,1,0:T(8,128)}, f32[4,8,128]{2,1,0:T(8,128)S(1)}, u32[]{:S(2)}) copy-start(f32[4,8,128]{2,1,0:T(8,128)S(1)} %pad_maximum_fusion.1) | copy-start | bytes 49156
  1924.9 1.5 copy-start.9
  1925.0 3.0 copy-start.8
  1925.9 3.9 copy-start.1
Sparse Core Ops, SparseCore 0:
  22.1 272.2 all-reduce.22
  753.7 134.3 all-reduce.24
  908.8 135.4 all-reduce.26
  1064.3 135.4 all-reduce.28
  1219.7 135.4 all-reduce.30
  1375.1 135.4 all-reduce.32
  1530.5 135.4 all-reduce.34
  1670.0 140.8 all-reduce.36
